TPU v7x, 512 devices: a whole 4x8x8 slice. The times are simulated.
512 devices in a mesh: dp: 32 (over x_lo, y, core), tensor: 16 (over x_hi, z).
Axes of the slice: x: 4 (x_hi: 2, x_lo: 2; x = x_hi * 2 + x_lo), y: 8, z: 8, core: 2. Of those that a mesh axis runs over, the one named last changes fastest.
Arguments:
- tokens: bfloat16 [8192, 4096], P(('dp', 'tensor')), may hold values from -110 to 110
- norm_gain: bfloat16 [4096], replicated, may hold values from 0.099609375 to 1.8984375
- query_weight: bfloat16 [4096, 4096], P('dp', 'tensor'), may hold values from -1 to 1
- kv_weight: bfloat16 [4096, 1024], P('dp', 'tensor'), may hold values from -1 to 1
- out_weight: bfloat16 [4096, 4096], P('tensor', 'dp'), may hold values from -0.09375 to 0.09375
- grad_out: bfloat16 [8192, 4096], P(('dp', 'tensor')), may hold values from -6 to 6
- doc_lengths: int32 [32, 4], P('dp'), may hold values from 1 to 128, 256 in all within a row
Outputs:
- input_grad: bfloat16 [8192, 4096], P(('dp', 'tensor'))
- query_weight_grad: float32 [4096, 4096], P('dp', 'tensor')
- kv_weight_grad: float32 [4096, 1024], P('dp', 'tensor')
Inputs may be any that keep to these rules, and one draw needn't show every extreme that they name: `doc_lengths`: each row sums to 256.
All inputs are finite; a program needn't handle non-finite values.
Results may differ from a plain program's by a relative error of at most 0.025.
Values may be sent and summed in bfloat16 or wider, within the bound.
A program may use at most 64 MiB of HBM per device.

v0:
```python
import math
import jax
import jax.numpy as jnp
from jax import lax
from jax.sharding import PartitionSpec as P

KVH = 4
HD = 128
epsilon = 1e-05


def partner_2(value, axis, bit):
    mask = 2**bit
    pairs = [(source, source ^ mask) for source in range(lax.axis_size(axis))]
    return lax.ppermute(value, axis, pairs)


def document_mask(lengths, length_total):
    ends = jnp.cumsum(lengths)
    positions = jnp.arange(length_total, dtype=jnp.int32)
    labels = jnp.sum((ends[None, :] <= positions[:, None]).astype(jnp.int32), axis=1)
    return (labels[:, None] == labels[None, :]) & (positions[None, :] <= positions[:, None])


def local(tokens, norm_gain, query_weight, kv_weight, out_weight, grad_out, doc_lengths):
    tensor_size = lax.axis_size("tensor")
    data_size = lax.axis_size("dp")
    tensor_index = lax.axis_index("tensor")
    sharers = tensor_size // KVH
    levels = sharers.bit_length() - 1
    contract_last = (((1,), (1,)), ((), ()))
    values32 = tokens.astype(jnp.float32)
    root_mean = jnp.sqrt(jnp.mean(values32 * values32, axis=-1) + epsilon)
    unit = values32 / root_mean[:, None]
    gain32 = norm_gain.astype(jnp.float32)
    normed_local = (unit * gain32).astype(jnp.bfloat16)
    normed = lax.all_gather(normed_local, "tensor", axis=0, tiled=True)
    seq_length = normed.shape[0]
    query_full = lax.all_gather(query_weight, "dp", axis=0, tiled=True)
    queries = jnp.dot(normed, query_full, preferred_element_type=jnp.float32).astype(jnp.bfloat16)
    kv_local = lax.all_gather(kv_weight, "dp", axis=0, tiled=True)
    head_weight = kv_local
    for bit_index in range(levels):
        partner = partner_2(head_weight, "tensor", bit_index)
        joined_upper_half = tensor_index >> bit_index & 1 == 1
        head_weight = jnp.concatenate(
            [
                jnp.where(joined_upper_half, partner, head_weight),
                jnp.where(joined_upper_half, head_weight, partner),
            ],
            axis=1,
        )
    keyvals = jnp.dot(normed, head_weight, preferred_element_type=jnp.float32).astype(jnp.bfloat16)
    key_rows = keyvals[:, :HD]
    value_rows = keyvals[:, HD:]
    grad_full = lax.all_gather(grad_out, "tensor", axis=0, tiled=True)
    out_grad = lax.dot_general(
        grad_full,
        lax.all_gather(out_weight, "dp", axis=1, tiled=True),
        contract_last,
        preferred_element_type=jnp.float32,
    ).astype(jnp.bfloat16)
    local_heads = queries.shape[1] // HD
    query_heads = queries.reshape(seq_length, local_heads, HD)
    out_heads = out_grad.reshape(seq_length, local_heads, HD)
    allowed = document_mask(doc_lengths[0], seq_length)
    scores = jnp.einsum(
        "qhd,td->hqt", query_heads, key_rows, preferred_element_type=jnp.float32
    ) / math.sqrt(HD)
    scores = jnp.where(allowed[None, :, :], scores, -1e30)
    peak = jnp.max(scores, axis=-1, keepdims=True)
    expo = jnp.exp(scores - peak)
    probs = expo / jnp.sum(expo, axis=-1, keepdims=True)
    probs_low = probs.astype(jnp.bfloat16)
    prob_grad = jnp.einsum("qhd,td->hqt", out_heads, value_rows, preferred_element_type=jnp.float32)
    inner = jnp.sum(probs * prob_grad, axis=-1, keepdims=True)
    score_grad = (probs * (prob_grad - inner) / math.sqrt(HD)).astype(jnp.bfloat16)
    query_grad = jnp.einsum("hqt,td->qhd", score_grad, key_rows, preferred_element_type=jnp.float32)
    query_grad = query_grad.astype(jnp.bfloat16).reshape(seq_length, local_heads * HD)
    key_part = jnp.einsum(
        "hqt,qhd->td", score_grad, query_heads, preferred_element_type=jnp.float32
    )
    value_part = jnp.einsum("hqt,qhd->td", probs_low, out_heads, preferred_element_type=jnp.float32)
    kv_partial = jnp.concatenate([key_part, value_part], axis=1)
    for bit_index in reversed(range(levels)):
        half_cols = kv_partial.shape[1] // 2
        upper_half = tensor_index >> bit_index & 1 == 1
        lower_cols = kv_partial[:, :half_cols]
        higher_cols = kv_partial[:, half_cols:]
        kept = jnp.where(upper_half, higher_cols, lower_cols)
        handed = jnp.where(upper_half, lower_cols, higher_cols)
        kv_partial = kept + partner_2(handed.astype(jnp.bfloat16), "tensor", bit_index).astype(
            handed.dtype
        )
    kv_grad = kv_partial.astype(jnp.bfloat16)
    from_query = lax.dot_general(
        query_grad, query_full, contract_last, preferred_element_type=jnp.float32
    )
    from_kv = lax.dot_general(kv_grad, kv_local, contract_last, preferred_element_type=jnp.float32)
    normed_grad = lax.psum_scatter(
        (from_query + from_kv).astype(jnp.bfloat16), "tensor", scatter_dimension=0, tiled=True
    ).astype(jnp.float32)
    scaled = normed_grad * gain32
    correction = unit * jnp.mean(scaled * unit, axis=-1, keepdims=True)
    input_grad = (grad_out.astype(jnp.float32) + (scaled - correction) / root_mean[:, None]).astype(
        jnp.bfloat16
    )
    combined = jnp.concatenate([query_grad, kv_grad], axis=1)
    weight_grads = (
        lax.psum_scatter(
            lax.dot_general(
                normed, combined, (((0,), (0,)), ((), ())), preferred_element_type=jnp.float32
            ).astype(jnp.bfloat16),
            "dp",
            scatter_dimension=0,
            tiled=True,
        ).astype(jnp.float32)
        / data_size
    )
    query_width = query_weight.shape[1]
    return (input_grad, weight_grads[:, :query_width], weight_grads[:, query_width:])


def solution(mesh):
    placed = (
        P(("dp", "tensor"), None),
        P(),
        P("dp", "tensor"),
        P("dp", "tensor"),
        P("tensor", "dp"),
        P(("dp", "tensor"), None),
        P("dp", None),
    )
    return jax.shard_map(
        local,
        mesh=mesh,
        in_specs=placed,
        out_specs=(P(("dp", "tensor"), None), P("dp", "tensor"), P("dp", "tensor")),
        check_vma=False,
    )
```

profile of v0, /device:TPU:4, one launch (start us, length us, event | category | flops | bytes accessed | tf_op | source)
XLA Modules:
  0.0 718.5 jit_solution(1927866429500999006)
XLA Ops:
  7.2 0.0 all-gather.5.cloned.1.call-start
  7.2 1.1 fusion.22
  8.3 0.7 convert_element_type.68
  9.0 0.0 copy-done.5
  9.0 1.7 multiply_convert_fusion
  10.6 0.0 all-gather.5.cloned.1.call-update
  10.7 0.0 all-gather.9.cloned.1.call-start
  10.7 0.7 all-gather.9.cloned.1.call-update
  11.4 0.0 all-gather.11.cloned.1.call-start
  11.5 0.7 all-gather.11.cloned.1.call-update
  12.2 0.0 all-gather.7.cloned.1.call-start
  12.2 36.2 %all_gather.16 = bf16[4096,64]{0,1:T(8,128)(2,1)S(1)} all-gather(bf16[128,64]{0,1:T(8,128)(2,1)} %param.10), channel_id=1, replica_groups=mesh['dp'=32,'tensor'=16] {'dp'}, dimensions={0}, use_global_device_ids=true | all-gather | bytes 540672 | tf_op jit(solution)/shard_map/all_gather | solution.py:41
  48.4 4.2 collective-permute-start
  52.6 0.0 all-gather.7.cloned.1.call-update
  52.6 0.0 reduce-scatter.5.cloned.1.call-start
  52.7 0.0 copy-start.7
  52.7 12.9 %collective-permute-done = bf16[4096,64]{0,1:T(8,128)(2,1)S(1)} collective-permute-done((bf16[4096,64]{0,1:T(8,128)(2,1)S(1)}, bf16[4096,64]{0,1:T(8,128)(2,1)S(1)}, u32[]{:S(2)}, u32[]{:S(2)}) %collective-permute-start) | collective-permute-done | bytes 524320 | tf_op jit(solution)/shard_map/ppermute | solution.py:15
  65.6 0.1 broadcast_select_fusion.3
  65.7 1.1 pad_maximum_fusion
  66.8 5.8 collective-permute-start.1
  72.7 0.0 copy-done.7
  72.7 0.2 reduce-window.8
  72.9 0.1 convert_reduce_fusion
  73.0 0.1 fusion.26
  73.1 55.3 %collective-permute-done.1 = bf16[4096,128]{0,1:T(8,128)(2,1)S(1)} collective-permute-done((bf16[4096,128]{0,1:T(8,128)(2,1)}, bf16[4096,128]{0,1:T(8,128)(2,1)S(1)}, u32[]{:S(2)}, u32[]{:S(2)}) %collective-permute-start.1) | collective-permute-done | bytes 1048608 | tf_op jit(solution)/shard_map/ppermute | solution.py:15
  128.4 1.8 broadcast_select_fusion.1
  130.2 2.9 fusion.15
  133.1 0.0 copy-start.4
  133.1 0.0 copy-start.1
  133.1 82.9 %all-gather.9.cloned.1.call-done = bf16[256,4096]{1,0:T(8,128)(2,1)} async-done(((bf16[16,4096]{1,0:T(8,128)(2,1)}), bf16[256,4096]{1,0:T(8,128)(2,1)}) %all-gather.9.cloned.1.call-update) | async-done | bytes 2097168 | tf_op jit(solution)/shard_map/all_gather | solution.py:56
  216.0 69.3 %all-gather.11.cloned.1.call-done = bf16[256,4096]{1,0:T(8,128)(2,1)} async-done(((bf16[256,128]{1,0:T(8,128)(2,1)}), bf16[256,4096]{1,0:T(8,128)(2,1)}) %all-gather.11.cloned.1.call-update) | async-done | bytes 2097168 | tf_op jit(solution)/shard_map/all_gather | solution.py:59
  285.4 3.0 convolution_convert_fusion.2
  288.4 0.0 copy-done.4
  288.4 0.2 convolution_bitcast_fusion
  288.6 64.3 %all-gather.7.cloned.1.call-done = bf16[4096,256]{1,0:T(8,128)(2,1)} async-done(((bf16[128,256]{1,0:T(8,128)(2,1)}), bf16[4096,256]{1,0:T(8,128)(2,1)}) %all-gather.7.cloned.1.call-update) | async-done | bytes 2097168 | tf_op jit(solution)/shard_map/all_gather | solution.py:39
  352.9 0.0 copy-done.1
  352.9 2.5 convolution_convert_fusion.3
  355.4 1.2 fusion.39
  356.6 0.0 copy-start.9
  356.6 0.2 convolution_bitcast_fusion.2
  356.9 0.5 copy-done.8
  357.4 0.0 copy-done.9
  357.4 0.9 select_convert_fusion
  358.4 4.8 collective-permute-start.2
  363.1 1.5 convolution_convert_fusion.1
  364.6 2.7 collective-permute-done.2
  367.3 0.9 convert_add_fusion
  368.2 2.6 collective-permute-start.3
  370.8 0.0 copy-done
  370.8 0.8 fusion.42
  371.6 2.4 collective-permute-done.3
  374.0 2.1 fusion.2
  376.1 0.0 reduce-scatter.5.cloned.1.call-update
  376.1 0.0 reduce-scatter.7.cloned.1.call-start
  376.2 2.4 convolution_convert_fusion
  378.6 2.8 copy.38
  381.4 0.0 reduce-scatter.7.cloned.1.call-update
  381.4 204.1 %reduce-scatter.5.cloned.1.call-done = bf16[16,4096]{1,0:T(8,128)(2,1)} async-done(((bf16[256,4096]{1,0:T(8,128)(2,1)}), bf16[16,4096]{1,0:T(8,128)(2,1)}) %reduce-scatter.5.cloned.1.call-update) | async-done | bytes 131088 | tf_op jit(solution)/shard_map/reduce_scatter | solution.py:100
  585.5 1.1 multiply_reduce_fusion.1
  586.7 1.7 add_convert_fusion
  588.4 120.9 %reduce-scatter.7.cloned.1.call-done = bf16[128,320]{1,0:T(8,128)(2,1)} async-done(((bf16[4096,320]{1,0:T(8,128)(2,1)}), bf16[128,320]{1,0:T(8,128)(2,1)}) %reduce-scatter.7.cloned.1.call-update) | async-done | bytes 81936
  709.3 1.0 copy.39
  710.3 0.6 slice.29
  710.9 0.8 copy.30
  (16 shorter events, 0.1 us)
Async XLA Ops:
  7.2 123.0 %all-gather.5.cloned.1.call-start = ((), (), s32[]{:S(2)}) async-start(), calls=%async_computation.2 | async-start | bytes 2228224 | tf_op jit(solution)/shard_map/all_gather | solution.py:37
  8.3 0.7 copy-start.5
  10.7 205.4 %all-gather.9.cloned.1.call-start = ((), (), s32[]{:S(2)}) async-start(), calls=%async_computation.4 | async-start | bytes 2228224 | tf_op jit(solution)/shard_map/all_gather | solution.py:56
  11.4 274.0 %all-gather.11.cloned.1.call-start = ((), (), s32[]{:S(2)}) async-start(), calls=%async_computation.5 | async-start | bytes 2162688 | tf_op jit(solution)/shard_map/all_gather | solution.py:59
  12.2 340.8 %all-gather.7.cloned.1.call-start = ((), (), s32[]{:S(2)}) async-start(), calls=%async_computation.3 | async-start | bytes 2162688 | tf_op jit(solution)/shard_map/all_gather | solution.py:39
  48.4 17.2 %collective-permute-start = (bf16[4096,64]{0,1:T(8,128)(2,1)S(1)}, bf16[4096,64]{0,1:T(8,128)(2,1)S(1)}, u32[]{:S(2)}, u32[]{:S(2)}) collective-permute-start(bf16[4096,64]{0,1:T(8,128)(2,1)S(1)} %all_gather.16), channel_id=1, source_target_pairs={{0,1},{1,0},{2,3},{3,2},{4,5},{5,4},{6,7},{7,6},{8,9},{9,8},{10,11... | collective-permute-start | bytes 1572872 | tf_op jit(solution)/shard_map/ppermute | solution.py:15
  52.6 532.9 %reduce-scatter.5.cloned.1.call-start = ((), (), s32[]{:S(2)}) async-start(), calls=%async_computation.6 | async-start | bytes 2228224 | tf_op jit(solution)/shard_map/reduce_scatter | solution.py:100
  52.7 20.0 %copy-start.7 = (s32[1,4]{1,0:T(1,128)S(1)}, s32[1,4]{1,0:T(1,128)}, u32[]{:S(2)}) copy-start(s32[1,4]{1,0:T(1,128)} %param.13) | copy-start | bytes 52
  66.8 61.5 %collective-permute-start.1 = (bf16[4096,128]{0,1:T(8,128)(2,1)}, bf16[4096,128]{0,1:T(8,128)(2,1)S(1)}, u32[]{:S(2)}, u32[]{:S(2)}) collective-permute-start(bf16[4096,128]{0,1:T(8,128)(2,1)} %pad_maximum_fusion), channel_id=1, source_target_pairs={{0,2},{1,3},{2,0},{3,1},{4,6},{5,7},{6,4},{7,5},{8,10},{9,11},{10,... | collective-permute-start | bytes 3145736 | tf_op jit(solution)/shard_map/ppermute | solution.py:15
  133.1 155.2 %copy-start.4 = (bf16[256,256]{1,0:T(8,128)(2,1)}, bf16[256,256]{1,0:T(8,128)(2,1)S(1)}, u32[]{:S(2)}) copy-start(bf16[256,256]{1,0:T(8,128)(2,1)S(1)} %fusion.15) | copy-start | bytes 393220
  133.1 219.8 %copy-start.1 = (bf16[256,4096]{1,0:T(8,128)(2,1)S(1)}, bf16[256,4096]{1,0:T(8,128)(2,1)}, u32[]{:S(2)}) copy-start(bf16[256,4096]{1,0:T(8,128)(2,1)} %all-gather.5.cloned.1.call-done) | copy-start | bytes 6291460
  356.6 0.8 copy-start.8
  356.6 0.8 copy-start.9
  358.4 12.5 %copy-start = (bf16[4096,256]{1,0:T(8,128)(2,1)S(1)}, bf16[4096,256]{1,0:T(8,128)(2,1)}, u32[]{:S(2)}) copy-start(bf16[4096,256]{1,0:T(8,128)(2,1)} %all-gather.7.cloned.1.call-done) | copy-start | bytes 6291460
  358.4 9.0 %collective-permute-start.2 = (bf16[256,128]{0,1:T(8,128)(2,1)}, bf16[256,128]{0,1:T(8,128)(2,1)}, u32[]{:S(2)}, u32[]{:S(2)}) collective-permute-start(bf16[256,128]{0,1:T(8,128)(2,1)} %get-tuple-element.18), channel_id=1, source_target_pairs={{0,2},{1,3},{2,0},{3,1},{4,6},{5,7},{6,4},{7,5},{8,10},{9,11},{10,... | collective-permute-start | bytes 196616 | tf_op jit(solution)/shard_map/ppermute | solution.py:15
  368.2 5.8 collective-permute-start.3
  376.1 333.2 %reduce-scatter.7.cloned.1.call-start = ((), (), s32[]{:S(2)}) async-start(), calls=%async_computation.7 | async-start | bytes 3244032
  381.4 204.1 %copy-start.2 = (bf16[16,4096]{1,0:T(8,128)(2,1)S(1)}, bf16[16,4096]{1,0:T(8,128)(2,1)}, u32[]{:S(2)}) copy-start(bf16[16,4096]{1,0:T(8,128)(2,1)} %param.7) | copy-start | bytes 393220
  381.4 204.1 %copy-start.6 = (f32[16]{0:T(128)S(1)}, f32[16]{0:T(128)}, u32[]{:S(2)}) copy-start(f32[16]{0:T(128)} %copy-done.5) | copy-start | bytes 196
  381.4 205.3 %copy-start.3 = (bf16[16,4096]{1,0:T(8,128)(2,1)S(1)}, bf16[16,4096]{1,0:T(8,128)(2,1)}, u32[]{:S(2)}) copy-start(bf16[16,4096]{1,0:T(8,128)(2,1)} %param.12) | copy-start | bytes 393220
Sparse Core Ops, SparseCore 0:
  11.7 109.4 all-gather.4
  124.4 91.6 all-gather.8
  218.1 67.2 all-gather.10
  287.4 65.4 all-gather.6
  376.2 209.2 reduce-scatter.4
  588.2 121.0 reduce-scatter.6
where the time goes:
time: 719 us
  waiting for transfers between devices  616 us (86%)
  blocking collectives  36.2 us (5%)
  matrix products  17.7 us (2%)
  starting transfers between devices  17.6 us (2%)
  between operations  14.3 us (2%)
  other arithmetic  10.6 us (1%)
    reduce_scatter x1, waiting for transfers between devices, local(): lax.psum_scatter((from_query + from_kv).astype(jnp.bfloat16), 'tensor', s...  204 us
    unnamed x7, waiting for transfers between devices  122 us
    all_gather x1, waiting for transfers between devices, local(): grad_full = lax.all_gather(grad_out, 'tensor', axis=0, tiled=True)  82.9 us
    ppermute x4, waiting for transfers between devices, partner_2(): return lax.ppermute(value, axis, pairs)  73.3 us
    all_gather x1, waiting for transfers between devices, local(): lax.all_gather(out_weight, 'dp', axis=1, tiled=True)  69.3 us
    all_gather x1, waiting for transfers between devices, local(): query_full = lax.all_gather(query_weight, 'dp', axis=0, tiled=True)  64.3 us
    all_gather x1, blocking collectives, local(): kv_local = lax.all_gather(kv_weight, 'dp', axis=0, tiled=True)  36.2 us
    ppermute x4, starting transfers between devices, partner_2(): return lax.ppermute(value, axis, pairs)  17.4 us
  transfers between devices with their start and end apart: 10, of which 9 were waited for; matrix products, arithmetic and copies ran while one was open for 3% of the time, Pallas kernels for 0%

commit v1 on v0

--- a/solution.py
+++ b/solution.py
@@ -56,7 +56,10 @@
     grad_full = lax.all_gather(grad_out, "tensor", axis=0, tiled=True)
     out_grad = lax.dot_general(
         grad_full,
-        lax.all_gather(out_weight, "dp", axis=1, tiled=True),
+        jnp.concatenate(
+            lax.all_to_all(jnp.stack([out_weight for _ in range(lax.axis_size("dp"))]), "dp", 0, 0),
+            axis=1,
+        ),
         contract_last,
         preferred_element_type=jnp.float32,
     ).astype(jnp.bfloat16)

time: 719 us -> 648 us (0.901)
  waiting for transfers between devices: 616 us -> 539 us
    all_gather x1 -> x0, waiting for transfers between devices: 69.3 us -> none  [local(): lax.all_gather(out_weight, 'dp', axis=1, tiled=True)]
    ppermute x4, waiting for transfers between devices: 73.3 us -> 66 us  [partner_2(): return lax.ppermute(value, axis, pairs)]
    unnamed x7 -> x6, waiting for transfers between devices: 122 us -> 122 us
  transfers between devices with their start and end apart: 10 -> 10, of which waited for: 9 -> 8; matrix products, arithmetic and copies ran while one was open for 3% -> 4% of each run, Pallas kernels for 0% -> 0%
where the time goes in v1:
time: 648 us
  waiting for transfers between devices  539 us (83%)
  blocking collectives  36.2 us (6%)
  starting transfers between devices  21.6 us (3%)
  matrix products  16.4 us (3%)
  between operations  14 us (2%)
  other arithmetic  12 us (2%)
  local copies, waits for them, and re-layouts  8.27 us (1%)
    reduce_scatter x1, waiting for transfers between devices, local(): lax.psum_scatter((from_query + from_kv).astype(jnp.bfloat16), 'tensor', s...  204 us
    unnamed x6, waiting for transfers between devices  122 us
    all_gather x1, waiting for transfers between devices, local(): grad_full = lax.all_gather(grad_out, 'tensor', axis=0, tiled=True)  81.9 us
    ppermute x4, waiting for transfers between devices, partner_2(): return lax.ppermute(value, axis, pairs)  66 us
    all_gather x1, waiting for transfers between devices, local(): query_full = lax.all_gather(query_weight, 'dp', axis=0, tiled=True)  65.2 us
    all_gather x1, blocking collectives, local(): kv_local = lax.all_gather(kv_weight, 'dp', axis=0, tiled=True)  36.2 us
    ppermute x4, starting transfers between devices, partner_2(): return lax.ppermute(value, axis, pairs)  17.3 us
  transfers between devices with their start and end apart: 10, of which 8 were waited for; matrix products, arithmetic and copies ran while one was open for 4% of the time, Pallas kernels for 0%

profile of v1, /device:TPU:4, one launch (start us, length us, event | category | flops | bytes accessed | tf_op | source)
XLA Modules:
  0.0 647.5 jit_solution(18058437337988467007)
XLA Ops:
  7.2 0.0 all-gather.4.cloned.1.call-start
  7.2 0.7 convert_element_type.68
  7.9 1.0 fusion.22
  9.0 1.7 multiply_convert_fusion
  10.6 0.0 all-gather.4.cloned.1.call-update
  10.7 0.0 all-gather.8.cloned.1.call-start
  10.7 0.7 all-gather.8.cloned.1.call-update
  11.4 36.2 %all_gather.13 = bf16[4096,64]{0,1:T(8,128)(2,1)S(1)} all-gather(bf16[128,64]{0,1:T(8,128)(2,1)} %param.10), channel_id=1, replica_groups=mesh['dp'=32,'tensor'=16] {'dp'}, dimensions={0}, use_global_device_ids=true | all-gather | bytes 540672 | tf_op jit(solution)/shard_map/all_gather | solution.py:41
  47.6 0.0 copy-start.1
  47.6 4.3 collective-permute-start
  51.9 0.9 copy.34
  52.9 1.6 stack.2
  54.5 0.0 copy-done.1
  54.5 4.0 all-to-all-start
  58.5 0.0 all-gather.6.cloned.1.call-start
  58.5 0.7 all-gather.6.cloned.1.call-update
  59.2 0.0 reduce-scatter.5.cloned.1.call-start
  59.3 0.0 copy-start.5
  59.3 5.9 collective-permute-done
  65.1 1.3 broadcast_select_fusion.3
  66.4 1.0 pad_maximum_fusion
  67.5 5.7 collective-permute-start.1
  73.1 0.0 copy-done.5
  73.1 0.2 reduce-window.8
  73.3 0.1 convert_reduce_fusion
  73.4 0.1 fusion.26
  73.5 55.4 %collective-permute-done.1 = bf16[4096,128]{0,1:T(8,128)(2,1)} collective-permute-done((bf16[4096,128]{0,1:T(8,128)(2,1)}, bf16[4096,128]{0,1:T(8,128)(2,1)}, u32[]{:S(2)}, u32[]{:S(2)}) %collective-permute-start.1) | collective-permute-done | bytes 1048608 | tf_op jit(solution)/shard_map/ppermute | solution.py:15
  128.9 3.0 broadcast_select_fusion.1
  131.9 2.9 fusion.15
  134.8 81.9 %all-gather.8.cloned.1.call-done = bf16[256,4096]{1,0:T(8,128)(2,1)} async-done(((bf16[16,4096]{1,0:T(8,128)(2,1)}), bf16[256,4096]{1,0:T(8,128)(2,1)}) %all-gather.8.cloned.1.call-update) | async-done | bytes 2097168 | tf_op jit(solution)/shard_map/all_gather | solution.py:56
  216.7 0.0 all-to-all-done
  216.7 2.5 convolution_convert_fusion.2
  219.3 0.2 convolution_bitcast_fusion
  219.5 65.2 %all-gather.6.cloned.1.call-done = bf16[4096,256]{1,0:T(8,128)(2,1)} async-done(((bf16[128,256]{1,0:T(8,128)(2,1)}), bf16[4096,256]{1,0:T(8,128)(2,1)}) %all-gather.6.cloned.1.call-update) | async-done | bytes 2097168 | tf_op jit(solution)/shard_map/all_gather | solution.py:39
  284.6 3.1 convolution_convert_fusion.3
  287.8 0.3 fusion.39
  288.1 0.2 convolution_bitcast_fusion.2
  288.4 0.5 copy-done.6
  288.9 0.3 select_convert_fusion
  289.2 0.0 copy-start
  289.2 4.8 collective-permute-start.2
  294.0 1.5 convolution_convert_fusion.1
  295.5 2.4 collective-permute-done.2
  297.9 2.6 collective-permute-start.3
  300.5 0.0 copy-done
  300.6 0.0 copy-start.2
  300.6 0.8 fusion.42
  301.3 2.4 collective-permute-done.3
  303.7 0.0 copy-done.2
  303.7 2.1 fusion.2
  305.8 0.0 reduce-scatter.5.cloned.1.call-update
  305.9 0.0 reduce-scatter.7.cloned.1.call-start
  305.9 2.4 convolution_convert_fusion
  308.4 2.8 copy.48
  311.1 0.0 reduce-scatter.7.cloned.1.call-update
  311.2 204.0 %reduce-scatter.5.cloned.1.call-done = bf16[16,4096]{1,0:T(8,128)(2,1)} async-done(((bf16[256,4096]{1,0:T(8,128)(2,1)}), bf16[16,4096]{1,0:T(8,128)(2,1)}) %reduce-scatter.5.cloned.1.call-update) | async-done | bytes 131088 | tf_op jit(solution)/shard_map/reduce_scatter | solution.py:103
  515.2 0.0 copy-done.3
  515.2 1.1 multiply_reduce_fusion.1
  516.3 0.0 copy-done.4
  516.3 1.7 add_convert_fusion
  518.0 120.5 %reduce-scatter.7.cloned.1.call-done = bf16[128,320]{1,0:T(8,128)(2,1)} async-done(((bf16[4096,320]{1,0:T(8,128)(2,1)}), bf16[128,320]{1,0:T(8,128)(2,1)}) %reduce-scatter.7.cloned.1.call-update) | async-done | bytes 81936
  638.6 1.0 copy.49
  639.6 0.6 slice.29
  640.3 0.8 copy.40
  (11 shorter events, 0.1 us)
Async XLA Ops:
  7.2 124.7 %all-gather.4.cloned.1.call-start = ((), (), s32[]{:S(2)}) async-start(), calls=%async_computation.3 | async-start | bytes 2228224 | tf_op jit(solution)/shard_map/all_gather | solution.py:37
  10.7 206.1 %all-gather.8.cloned.1.call-start = ((), (), s32[]{:S(2)}) async-start(), calls=%async_computation.5 | async-start | bytes 2228224 | tf_op jit(solution)/shard_map/all_gather | solution.py:56
  47.6 6.8 %copy-start.1 = (bf16[4096,64]{0,1:T(8,128)(2,1)}, bf16[4096,64]{0,1:T(8,128)(2,1)S(1)}, u32[]{:S(2)}) copy-start(bf16[4096,64]{0,1:T(8,128)(2,1)S(1)} %all_gather.13) | copy-start | bytes 1572868
  47.6 17.5 %collective-permute-start = (bf16[4096,64]{0,1:T(8,128)(2,1)S(1)}, bf16[4096,64]{0,1:T(8,128)(2,1)}, u32[]{:S(2)}, u32[]{:S(2)}) collective-permute-start(bf16[4096,64]{0,1:T(8,128)(2,1)S(1)} %all_gather.13), channel_id=1, source_target_pairs={{0,1},{1,0},{2,3},{3,2},{4,5},{5,4},{6,7},{7,6},{8,9},{9,8},{10,11... | collective-permute-start | bytes 1572872 | tf_op jit(solution)/shard_map/ppermute | solution.py:15
  54.5 162.3 %all-to-all-start = ((bf16[32,256,128]{1,2,0:T(8,128)(2,1)}), bf16[32,256,128]{1,2,0:T(8,128)(2,1)S(1)}, u32[]{:S(2)}, u32[]{:S(2)}) async-start(bf16[32,256,128]{1,2,0:T(8,128)(2,1)} %stack.2), calls=%async_computation | async-start | bytes 4194304 | tf_op jit(solution)/shard_map/all_to_all | solution.py:60
  58.5 226.2 %all-gather.6.cloned.1.call-start = ((), (), s32[]{:S(2)}) async-start(), calls=%async_computation.4 | async-start | bytes 2162688 | tf_op jit(solution)/shard_map/all_gather | solution.py:39
  59.2 456.0 %reduce-scatter.5.cloned.1.call-start = ((), (), s32[]{:S(2)}) async-start(), calls=%async_computation.6 | async-start | bytes 2228224 | tf_op jit(solution)/shard_map/reduce_scatter | solution.py:103
  59.3 13.9 %copy-start.5 = (s32[1,4]{1,0:T(1,128)S(1)}, s32[1,4]{1,0:T(1,128)}, u32[]{:S(2)}) copy-start(s32[1,4]{1,0:T(1,128)} %param.13) | copy-start | bytes 52
  67.5 61.4 %collective-permute-start.1 = (bf16[4096,128]{0,1:T(8,128)(2,1)}, bf16[4096,128]{0,1:T(8,128)(2,1)}, u32[]{:S(2)}, u32[]{:S(2)}) collective-permute-start(bf16[4096,128]{0,1:T(8,128)(2,1)} %pad_maximum_fusion), channel_id=1, source_target_pairs={{0,2},{1,3},{2,0},{3,1},{4,6},{5,7},{6,4},{7,5},{8,10},{9,11},{10,... | collective-permute-start | bytes 3145736 | tf_op jit(solution)/shard_map/ppermute | solution.py:15
  288.1 0.8 copy-start.6
  289.2 11.3 %copy-start = (bf16[4096,256]{1,0:T(8,128)(2,1)S(1)}, bf16[4096,256]{1,0:T(8,128)(2,1)}, u32[]{:S(2)}) copy-start(bf16[4096,256]{1,0:T(8,128)(2,1)} %all-gather.6.cloned.1.call-done) | copy-start | bytes 6291460
  289.2 8.7 %collective-permute-start.2 = (bf16[256,128]{0,1:T(8,128)(2,1)S(1)}, bf16[256,128]{0,1:T(8,128)(2,1)S(1)}, u32[]{:S(2)}, u32[]{:S(2)}) collective-permute-start(bf16[256,128]{0,1:T(8,128)(2,1)S(1)} %get-tuple-element.21), channel_id=1, source_target_pairs={{0,2},{1,3},{2,0},{3,1},{4,6},{5,7},{6,4},{7,5},{8,10},{9,11},{10,... | collective-permute-start | bytes 196616 | tf_op jit(solution)/shard_map/ppermute | solution.py:15
  297.9 5.8 collective-permute-start.3
  300.6 3.2 copy-start.2
  305.9 332.7 %reduce-scatter.7.cloned.1.call-start = ((), (), s32[]{:S(2)}) async-start(), calls=%async_computation.7 | async-start | bytes 3244032
  311.1 204.1 %copy-start.3 = (bf16[16,4096]{1,0:T(8,128)(2,1)S(1)}, bf16[16,4096]{1,0:T(8,128)(2,1)}, u32[]{:S(2)}) copy-start(bf16[16,4096]{1,0:T(8,128)(2,1)} %param.7) | copy-start | bytes 393220
  311.1 205.2 %copy-start.4 = (bf16[16,4096]{1,0:T(8,128)(2,1)S(1)}, bf16[16,4096]{1,0:T(8,128)(2,1)}, u32[]{:S(2)}) copy-start(bf16[16,4096]{1,0:T(8,128)(2,1)} %param.12) | copy-start | bytes 393220
Sparse Core Ops, SparseCore 0:
  11.7 109.5 all-gather.3
  124.5 92.1 all-gather.7
  218.9 65.6 all-gather.5
  306.0 209.1 reduce-scatter.4
  517.9 120.6 reduce-scatter.6
